TPU v7x, 32 devices: a whole 2x2x4 slice. The times are simulated.
32 devices in a mesh: wide: 8 (over y, x, core), narrow: 4 (over z).
Axes of the slice: x: 2, y: 2, z: 4, core: 2. Of those that a mesh axis runs over, the one named last changes fastest.
Arguments:
- pooled: bfloat16 [16384, 1024], P(('wide', 'narrow')), may hold values from -6 to 6
- cotangent: bfloat16 [16384, 512], P(('wide', 'narrow')), may hold values from -6 to 6
- w_first: bfloat16 [1024, 1024], P('narrow'), may hold values from -0.1875 to 0.1875
- b_first: float32 [1024], replicated, may hold values from -5 to 5
- w_second: bfloat16 [1024, 512], P('narrow'), may hold values from -0.1875 to 0.1875
- counts: bfloat16 [8, 64, 16384], P(None, 'narrow', 'wide'), may hold values from 0 to 3, as said below
- row_ids: int32 [8, 64], P(None, 'narrow'), may hold values from 0 to 63, as said below
- table: float32 [8, 256, 128], P(None, 'narrow'), may hold values from -6 to 6
- accum: float32 [8, 256, 128], P(None, 'narrow'), may hold values from 0.1 to 10
Outputs:
- new_table: float32 [8, 256, 128], P(None, 'narrow')
- new_accum: float32 [8, 256, 128], P(None, 'narrow')
Inputs may be any that keep to these rules, and one draw needn't show every extreme that they name: `counts`: each entry is zero where the sample does not look up the active row, else a positive lookup weight. `row_ids`: for each table, the 16 ids of one owner (slots j * 16 to (j + 1) * 16 - 1) are distinct.
All inputs are finite; a program needn't handle non-finite values.
Results may differ from a plain program's by a relative error of at most 0.0038.
Values may be sent and summed in bfloat16 or wider, within the bound.
A program may use at most 128 MiB of HBM per device.

v0:
```python
import math

import jax
import jax.numpy as jnp
from jax import lax
from jax.sharding import PartitionSpec as P

clip_factor = 0.5
learn_rate = 0.05
epsilon = 1e-08


def tower_back(inputs, cotangent, w_first, b_first, w_second):
    hidden_in = jnp.dot(inputs, w_first, preferred_element_type=jnp.float32) + b_first
    back_hidden = lax.dot_general(
        cotangent, w_second, (((1,), (1,)), ((), ())), preferred_element_type=jnp.float32
    )
    sigmoid_val = jax.nn.sigmoid(hidden_in)
    slopes = sigmoid_val * (1.0 + hidden_in * (1.0 - sigmoid_val))
    deltas = (back_hidden * slopes).astype(jnp.bfloat16)
    return lax.dot_general(
        deltas, w_first, (((1,), (1,)), ((), ())), preferred_element_type=jnp.float32
    ).astype(jnp.bfloat16)


def clip_rows(grads, limit):
    norms = jnp.sqrt(jnp.sum(grads * grads, axis=-1, keepdims=True))
    return grads * (limit / jnp.maximum(norms, limit))


def adagrad_rows(current, old_acc, summed):
    new_acc = old_acc + summed * summed
    return (current - learn_rate * summed / (jnp.sqrt(new_acc) + epsilon), new_acc)


def shards(pooled, cotangent, w_first, b_first, w_second, counts, row_ids, table, accum):
    full_first, full_second = (
        lax.all_gather(w_first, "narrow", axis=0, tiled=True),
        lax.all_gather(w_second, "narrow", axis=0, tiled=True),
    )
    grad_in = tower_back(pooled, cotangent, full_first, b_first, full_second)
    tables = counts.shape[0]
    slots = counts.shape[1]
    bags = counts.shape[2]
    emb = table.shape[2]
    samples = pooled.shape[0]
    scale = 1.0 / math.sqrt(bags)
    limit = clip_factor * math.sqrt(emb)
    regrouped = lax.all_to_all(counts, "narrow", split_axis=2, concat_axis=1, tiled=True)
    local_grad = grad_in.reshape(samples, tables, emb)
    grads = lax.psum_scatter(
        jnp.einsum(
            "tab,btd->atd", regrouped, local_grad, preferred_element_type=jnp.float32
        ).reshape(slots * lax.axis_size("narrow"), tables * emb),
        "narrow",
        scatter_dimension=0,
        tiled=True,
    ).reshape(slots, tables, emb)
    clipped = clip_rows(grads * scale, limit)
    table_index = jnp.arange(tables, dtype=jnp.int32)[:, None]
    current = jnp.transpose(table[table_index, row_ids], (1, 0, 2))
    old_acc = jnp.transpose(accum[table_index, row_ids], (1, 0, 2))
    summed = lax.psum(clipped, "wide")
    new_rows, new_acc = adagrad_rows(current, old_acc, summed)
    new_table = table.at[table_index, row_ids].set(jnp.transpose(new_rows, (1, 0, 2)))
    new_accum = accum.at[table_index, row_ids].set(jnp.transpose(new_acc, (1, 0, 2)))
    return (new_table, new_accum)


def solution(mesh):
    in_specs = (
        P(("wide", "narrow"), None),
        P(("wide", "narrow"), None),
        P("narrow", None),
        P(),
        P("narrow", None),
        P(None, "narrow", "wide"),
        P(None, "narrow"),
        P(None, "narrow", None),
        P(None, "narrow", None),
    )
    out_specs = (P(None, "narrow", None), P(None, "narrow", None))
    return jax.shard_map(shards, mesh=mesh, in_specs=in_specs, out_specs=out_specs, check_vma=False)
```

profile of v0, /device:TPU:0, one launch (start us, length us, event | category | flops | bytes accessed | tf_op | source)
XLA Modules:
  0.0 199.6 jit_solution(9209073839710677612)
XLA Ops:
  7.2 0.0 all-gather.5.cloned.1.call-start
  7.2 1.1 copy.53
  8.3 0.9 copy.54
  9.3 0.0 all-gather.3.cloned.1.call-start
  9.3 0.7 all-gather.3.cloned.1.call-update
  10.0 0.0 reduce-scatter.2.cloned.1.call-start
  10.1 4.2 %copy.26 = bf16[8,16,2048]{1,0,2:T(8,128)(2,1)} copy(bf16[8,16,2048]{2,1,0:T(8,128)(2,1)S(1)} %copy-done.3) | data formatting | bytes 1048576 | tf_op args[5]
  14.3 5.8 %reshape.51 = bf16[4,2,32768]{2,1,0:T(2,128)(2,1)S(1)} reshape(bf16[2048,8,16]{2,1,0:T(8,128)(2,1)} %bitcast.58) | data formatting | bytes 1048576
  20.1 35.4 %all_to_all.18 = bf16[4,2,32768]{2,1,0:T(2,128)(2,1)S(1)} all-to-all(bf16[4,2,32768]{2,1,0:T(2,128)(2,1)S(1)} %reshape.51), channel_id=1, replica_groups=mesh['wide'=8,'narrow'=4] {'narrow'}, dimensions={0} | all-to-all | bytes 1048576 | tf_op jit(solution)/shard_map/all_to_all | solution.py:49
  55.5 4.1 %reshape.52 = bf16[2048,8,16]{2,1,0:T(8,128)(2,1)} reshape(bf16[4,2,32768]{2,1,0:T(2,128)(2,1)S(1)} %all_to_all.18) | data formatting | bytes 1048576
  59.7 4.4 %copy.27 = bf16[8,16,4,512]{3,1,2,0:T(8,128)(2,1)S(1)} copy(bf16[8,16,4,512]{1,0,3,2:T(8,128)(2,1)} %bitcast.57) | data formatting | bytes 1048576 | tf_op jit(solution)/shard_map/all_to_all | solution.py:49
  64.1 5.2 %all-gather.5.cloned.1.call-done = bf16[1024,1024]{1,0:T(8,128)(2,1)} async-done(((bf16[256,1024]{1,0:T(8,128)(2,1)}), bf16[1024,1024]{1,0:T(8,128)(2,1)}) %all-gather.5.cloned.1.call-update) | async-done | bytes 2097168 | tf_op jit(solution)/shard_map/all_gather | solution.py:38
  69.2 4.2 %fusion.13 = f32[512,1024]{1,0:T(8,128)} fusion(bf16[512,1024]{1,0:T(8,128)(2,1)S(1)} %copy-done, bf16[1024,1024]{1,0:T(8,128)(2,1)} %all-gather.5.cloned.1.call-done), kind=kOutput, calls=%fused_computation.32 | convolution fusion | flops 1073741824 | bytes 5242880 | tf_op jit(solution)/shard_map/dot_general | solution.py:14
  73.4 24.1 %all-gather.3.cloned.1.call-done = bf16[1024,512]{1,0:T(8,128)(2,1)} async-done(((bf16[256,512]{1,0:T(8,128)(2,1)}), bf16[1024,512]{1,0:T(8,128)(2,1)}) %all-gather.3.cloned.1.call-update) | async-done | bytes 1048592 | tf_op jit(solution)/shard_map/all_gather | solution.py:39
  97.5 4.6 %fusion = bf16[64,8,8,128]{3,2,1,0:T(8,128)(2,1)S(1)} fusion(bf16[1024,1024]{1,0:T(8,128)(2,1)} %all-gather.5.cloned.1.call-done, f32[512,1024]{1,0:T(8,128)} %fusion.13, bf16[512,512]{1,0:T(8,128)(2,1)} %param.10, bf16[1024,512]{1,0:T(8,128)(2,1)} %all-gather.3.cloned.1.call-done, f32[1024]{0:T(1024)S(1)} %copy-done.5), kind=kOutput, calls=%fused_computation.6 | convolution fusion | flops 1616379904 | bytes 6819840 | tf_op jit(solution)/shard_map/dot_general | solution.py:21
  102.1 0.3 convolution_bitcast_fusion
  102.4 0.7 copy.47
  103.1 0.0 reduce-scatter.2.cloned.1.call-update
  103.1 0.0 all-reduce.2.cloned.1.call-start
  103.2 19.5 %reduce-scatter.2.cloned.1.call-done = f32[16,1024]{1,0:T(8,128)} async-done(((f32[64,1024]{1,0:T(8,128)}), f32[16,1024]{1,0:T(8,128)}) %reduce-scatter.2.cloned.1.call-update) | async-done | bytes 65552 | tf_op jit(solution)/shard_map/reduce_scatter | solution.py:51
  122.7 0.9 copy.35
  123.6 0.1 multiply_reduce_fusion
  123.7 0.7 bitcast_multiply_fusion
  124.4 0.1 reshape.27
  124.5 1.2 gather_fusion
  125.7 1.2 gather_fusion.1
  127.0 0.1 reshape.39
  127.1 50.5 %all-reduce.2.cloned.1.call-done = f32[16,8,128]{2,1,0:T(8,128)} async-done(((f32[16,8,128]{2,1,0:T(8,128)}), f32[16,8,128]{2,1,0:T(8,128)}) %all-reduce.2.cloned.1.call-update) | async-done | bytes 65552 | tf_op jit(solution)/shard_map/psum | solution.py:63
  177.6 0.9 fusion.6
  178.6 6.9 %scatter_fusion.1 = f32[8,64,128]{2,1,0:T(8,128)S(1)} fusion(f32[8,64,128]{2,1,0:T(8,128)S(1)} %copy.54, s32[128]{0:T(128)S(1)} %reshape.39, f32[128,128]{1,0:T(8,128)S(1)} %bitcast.64), kind=kCustom, calls=%fused_computation.3 | custom fusion | bytes 197632 | tf_op jit(solution)/shard_map/scatter | solution.py:66
  185.5 6.9 %scatter_fusion = f32[8,64,128]{2,1,0:T(8,128)S(1)} fusion(f32[8,64,128]{2,1,0:T(8,128)S(1)} %copy.53, s32[128]{0:T(128)S(1)} %reshape.39, f32[128,128]{1,0:T(8,128)S(1)} %bitcast.63), kind=kCustom, calls=%fused_computation.2 | custom fusion | bytes 197632 | tf_op jit(solution)/shard_map/scatter | solution.py:65
  192.4 0.7 copy-done.1
  (18 shorter events, 0.1 us)
Async XLA Ops:
  7.2 62.1 %copy-start = (bf16[512,1024]{1,0:T(8,128)(2,1)S(1)}, bf16[512,1024]{1,0:T(8,128)(2,1)}, u32[]{:S(2)}) copy-start(bf16[512,1024]{1,0:T(8,128)(2,1)} %param.9) | copy-start | bytes 3145732
  7.2 2.9 %copy-start.3 = (bf16[8,16,2048]{2,1,0:T(8,128)(2,1)S(1)}, bf16[8,16,2048]{2,1,0:T(8,128)(2,1)}, u32[]{:S(2)}) copy-start(bf16[8,16,2048]{2,1,0:T(8,128)(2,1)} %param.14) | copy-start | bytes 1572868
  7.2 62.0 %all-gather.5.cloned.1.call-start = ((), (), s32[]{:S(2)}) async-start(), calls=%async_computation.3 | async-start | bytes 2621440 | tf_op jit(solution)/shard_map/all_gather | solution.py:38
  9.3 88.2 %all-gather.3.cloned.1.call-start = ((), (), s32[]{:S(2)}) async-start(), calls=%async_computation.2 | async-start | bytes 1310720 | tf_op jit(solution)/shard_map/all_gather | solution.py:39
  10.0 112.6 %reduce-scatter.2.cloned.1.call-start = ((), (), s32[]{:S(2)}) async-start(), calls=%async_computation.4 | async-start | bytes 327680 | tf_op jit(solution)/shard_map/reduce_scatter | solution.py:51
  64.1 33.4 %copy-start.5 = (f32[1024]{0:T(1024)S(1)}, f32[1024]{0:T(1024)}, u32[]{:S(2)}) copy-start(f32[1024]{0:T(1024)} %param.12) | copy-start | bytes 12292
  102.0 22.4 %copy-start.4 = (s32[8,16]{1,0:T(8,128)S(1)}, s32[8,16]{1,0:T(8,128)}, u32[]{:S(2)}) copy-start(s32[8,16]{1,0:T(8,128)} %param.15) | copy-start | bytes 1540
  103.1 74.5 %all-reduce.2.cloned.1.call-start = ((), (), s32[]{:S(2)}) async-start(), calls=%async_computation.5 | async-start | bytes 131072 | tf_op jit(solution)/shard_map/psum | solution.py:63
  185.5 6.9 %copy-start.2 = (f32[8,64,128]{2,1,0:T(8,128)}, f32[8,64,128]{2,1,0:T(8,128)S(1)}, u32[]{:S(2)}) copy-start(f32[8,64,128]{2,1,0:T(8,128)S(1)} %scatter_fusion.1) | copy-start | bytes 786436
  192.4 0.7 copy-start.1
Sparse Core Ops, SparseCore 0:
  9.6 59.6 all-gather.4
  70.8 26.6 all-gather.2
  103.3 19.3 reduce-scatter.1
  126.2 51.3 all-reduce.1
where the time goes:
time: 200 us
  waiting for transfers between devices  100 us (50%)
  local copies, waits for them, and re-layouts  39.3 us (20%)
  blocking collectives  35.4 us (18%)
  between operations  13.9 us (7%)
  matrix products  9.06 us (5%)
    psum x1, waiting for transfers between devices, shards(): summed = lax.psum(clipped, 'wide')  50.5 us
    all_to_all x1, blocking collectives, shards(): lax.all_to_all(counts, 'narrow', split_axis=2, concat_axis=1, tiled=True)  35.4 us
    all_gather x1, waiting for transfers between devices, shards(): lax.all_gather(w_second, 'narrow', axis=0, tiled=True)  24.1 us
    reduce_scatter x1, waiting for transfers between devices, shards(): lax.psum_scatter(jnp.einsum('tab,btd->atd', regrouped, local_grad, prefer...  19.5 us
    unnamed x18, local copies, waits for them, and re-layouts  17.7 us
    scatter x1, local copies, waits for them, and re-layouts, shards(): accum.at[table_index, row_ids].set(jnp.transpose(new_acc, (1, 0, 2)))  6.9 us
    scatter x1, local copies, waits for them, and re-layouts, shards(): table.at[table_index, row_ids].set(jnp.transpose(new_rows, (1, 0, 2)))  6.9 us
    all_gather x1, waiting for transfers between devices, shards(): lax.all_gather(w_first, 'narrow', axis=0, tiled=True)  5.15 us
  transfers between devices with their start and end apart: 4, of which 4 were waited for; matrix products, arithmetic and copies ran while one was open for 13% of the time, Pallas kernels for 0%

commit v1 on v0

v1 whole, which is shorter than its diff:
```python
import functools
import math

import jax
import jax.numpy as jnp
from jax import lax
from jax.experimental import pallas as pl
from jax.experimental.pallas import tpu as pltpu
from jax.sharding import PartitionSpec as P

MESH = pl.DeviceIdType.MESH
clip_factor = 0.5
learn_rate = 0.05
epsilon = 1e-08
NT = (((1,), (1,)), ((), ()))


def flip(index, bit):
    return index + bit * (1 - 2 * ((index // bit) % 2))


def pieces_of(shard_rows, n_wide):
    pieces = 1
    while n_wide % (2 * pieces) == 0 and shard_rows % (32 * pieces) == 0:
        pieces *= 2
    return pieces


def orders_of(pieces):
    bits = []
    bit = pieces // 2
    while bit:
        bits.append(bit)
        bit //= 2
    swapped = list(bits)
    if len(bits) > 2:
        swapped[0], swapped[1] = bits[1], bits[0]
    return bits, swapped


def tower_kernel(
    n_wide, n_narrow, pieces, scale, limit,
    pooled_hbm, cot_hbm, w1_hbm, w2_hbm, bias_ref, counts_hbm, out_ref,
    pooled, cot, w1, w2, looks, hidden, back, deltas, gsend, grecv, cbuf, crecv, sums,
    local_sem, wsend_sem, wrecv_sem, csend_sem, crecv_sem, gsend_sem, grecv_sem,
    ssend_sem, srecv_sem, asend_sem, arecv_sem,
):
    wide = lax.axis_index("wide")
    narrow = lax.axis_index("narrow")
    shard = w1_hbm.shape[0]
    piece_rows = shard // pieces
    bags = pooled.shape[0]
    inner = w1.shape[1]
    emb = gsend.shape[2]
    tables, slots = looks.shape[1], looks.shape[2]
    rest = n_narrow - 1
    part = wide % pieces
    base = wide - part
    full = (w1, w2)
    shards = (w1_hbm, w2_hbm)
    orders = orders_of(pieces)
    stages = len(orders[0])

    def lane_block(index, size):
        return pl.ds(pl.multiple_of(index * size, size), size)

    def local(step, src, dst):
        return pltpu.make_async_copy(src, dst, local_sem.at[step])

    own_rows = lane_block(narrow, shard)
    locals_ = [
        local(0, pooled_hbm, pooled),
        local(1, w1_hbm, w1.at[own_rows, :]),
        local(2, cot_hbm, cot),
        local(3, w2_hbm, w2.at[own_rows, :]),
        local(4, counts_hbm.at[:, :, lane_block(narrow, bags)], looks.at[narrow]),
    ]
    for copy in locals_:
        copy.start()

    barrier = pltpu.get_barrier_semaphore()
    for d in range(1, n_narrow):
        pl.semaphore_signal(
            barrier, inc=1, device_id={"narrow": (narrow + d) % n_narrow}, device_id_type=MESH
        )
    for d in range(1, n_wide):
        pl.semaphore_signal(
            barrier, inc=1, device_id={"wide": (wide + d) % n_wide}, device_id_type=MESH
        )
    pl.semaphore_wait(barrier, n_narrow + n_wide - 2)

    def remote(src, dst, send, recv, device):
        return pltpu.make_async_remote_copy(
            src_ref=src, dst_ref=dst, send_sem=send, recv_sem=recv,
            device_id=device, device_id_type=MESH,
        )

    sent = []

    def launch(copy):
        copy.start()
        sent.append(copy)

    def rows_at(source, piece):
        return pl.ds(pl.multiple_of(source * shard + piece * piece_rows, piece_rows), piece_rows)

    for d in range(rest):
        target = {"narrow": (narrow + d + 1) % n_narrow}
        for m in range(2):
            launch(remote(
                shards[m].at[lane_block(part, piece_rows), :],
                full[m].at[rows_at(narrow, part), :],
                wsend_sem.at[m, d, 0], wrecv_sem.at[m, d, 0], target,
            ))
    for d in range(rest):
        owner = (narrow + d + 1) % n_narrow
        launch(remote(
            counts_hbm.at[:, :, lane_block(owner, bags)], looks.at[narrow],
            csend_sem.at[d], crecv_sem.at[d], {"narrow": owner},
        ))

    held = [[[part] for _ in range(rest)] for _ in range(2)]

    def stage_arrive(m, d, stage):
        source = (narrow + n_narrow - d - 1) % n_narrow
        if stage == 0:
            new = [part]
            device = {"narrow": source}
        else:
            bit = orders[m][stage - 1]
            new = [flip(q, bit) for q in held[m][d]]
            device = {"wide": base + flip(part, bit)}
        first = 0 if stage == 0 else len(held[m][d])
        for i, q in enumerate(new):
            view = full[m].at[rows_at(source, q), :]
            remote(
                view, view, wsend_sem.at[m, d, first + i], wrecv_sem.at[m, d, first + i], device
            ).wait_recv()
        if stage:
            held[m][d] = held[m][d] + new

    def stage_send(m, d, stage):
        source = (narrow + n_narrow - d - 1) % n_narrow
        bit = orders[m][stage]
        device = {"wide": base + flip(part, bit)}
        first = len(held[m][d])
        for i, q in enumerate(held[m][d]):
            view = full[m].at[rows_at(source, q), :]
            launch(remote(
                view, view, wsend_sem.at[m, d, first + i], wrecv_sem.at[m, d, first + i], device
            ))

    tile = min(256, inner)

    def add_chunk(source, fresh):
        rows = lane_block(source, shard)
        lhs = pooled[:, rows]

        def body(t, carry):
            columns = lane_block(t, tile)
            value = jnp.dot(lhs, w1[rows, columns], preferred_element_type=jnp.float32)
            if fresh:
                hidden[:, columns] = value
            else:
                hidden[:, columns] = hidden[:, columns] + value
            return carry

        lax.fori_loop(0, inner // tile, body, 0)
        back[:, rows] = lax.dot_general(
            cot[...], w2[rows, :], NT, preferred_element_type=jnp.float32
        )

    chunked = shard % 128 == 0
    for copy in locals_:
        copy.wait()
    if chunked:
        add_chunk(narrow, True)
    for t in range(rest + stages):
        for stage in range(stages + 1):
            d = t - stage
            if 0 <= d < rest:
                for m in range(2):
                    stage_arrive(m, d, stage)
                    if stage < stages:
                        stage_send(m, d, stage)
        d = t - stages
        if chunked and 0 <= d < rest:
            add_chunk((narrow + n_narrow - d - 1) % n_narrow, False)

    def activate(t, carry):
        columns = lane_block(t, tile)
        if chunked:
            value = hidden[:, columns]
            back_value = back[:, columns]
        else:
            value = jnp.dot(pooled[...], w1[:, columns], preferred_element_type=jnp.float32)
            back_value = lax.dot_general(
                cot[...], w2[columns, :], NT, preferred_element_type=jnp.float32
            )
        value = value + bias_ref[:, columns]
        sig = jax.nn.sigmoid(value)
        slopes = sig * (1.0 + value * (1.0 - sig))
        deltas[:, columns] = (back_value * slopes).astype(jnp.bfloat16)
        return carry

    lax.fori_loop(0, inner // tile, activate, 0)

    for d in range(rest):
        source = (narrow + n_narrow - d - 1) % n_narrow
        view = looks.at[source]
        remote(view, view, csend_sem.at[d], crecv_sem.at[d], {"narrow": source}).wait_recv()

    group = max(1, 256 // emb)
    groups = tables // group
    for t in range(groups):
        wrows = w1[t * group * emb:(t + 1) * group * emb, :]
        grad_in = lax.dot_general(
            deltas[...], wrows, NT, preferred_element_type=jnp.float32
        ).astype(jnp.bfloat16)
        for i in range(group):
            k = t * group + i
            lookups = looks[:, k].reshape(n_narrow * slots, bags)
            value = jnp.dot(
                lookups, grad_in[:, i * emb:(i + 1) * emb], preferred_element_type=jnp.float32
            )
            for owner in range(n_narrow):
                gsend[owner, k * slots:(k + 1) * slots, :] = value[owner * slots:(owner + 1) * slots]
        block = pl.ds(t * group * slots, group * slots)
        for d in range(rest):
            owner = (narrow + d + 1) % n_narrow
            launch(remote(
                gsend.at[owner, block, :], grecv.at[narrow, block, :],
                gsend_sem.at[d, t], grecv_sem.at[d, t], {"narrow": owner},
            ))
    total = gsend[narrow]
    for d in range(rest):
        source = (narrow + n_narrow - d - 1) % n_narrow
        for t in range(groups):
            view = grecv.at[source, pl.ds(t * group * slots, group * slots), :]
            remote(view, view, gsend_sem.at[d, t], grecv_sem.at[d, t], {"narrow": source}).wait_recv()
        total = total + grecv[source]
    grads = total * scale
    norms = jnp.sqrt(jnp.sum(grads * grads, axis=-1, keepdims=True))
    clipped = grads * (limit / jnp.maximum(norms, limit))
    span = cbuf.shape[1]
    for i in range(n_wide):
        cbuf[i] = clipped[i * span:(i + 1) * span]
    for e in range(n_wide - 1):
        target = (wide + e + 1) % n_wide
        launch(remote(
            cbuf.at[target], crecv.at[wide], ssend_sem.at[e], srecv_sem.at[e], {"wide": target}
        ))
    summed = cbuf[wide]
    for e in range(n_wide - 1):
        source = (wide + n_wide - e - 1) % n_wide
        view = crecv.at[source]
        remote(view, view, ssend_sem.at[e], srecv_sem.at[e], {"wide": source}).wait_recv()
        summed = summed + crecv[source]
    sums[wide] = summed
    for e in range(n_wide - 1):
        target = (wide + e + 1) % n_wide
        launch(remote(
            sums.at[wide], sums.at[wide], asend_sem.at[e], arecv_sem.at[e], {"wide": target}
        ))
    for e in range(n_wide - 1):
        source = (wide + n_wide - e - 1) % n_wide
        view = sums.at[source]
        remote(view, view, asend_sem.at[e], arecv_sem.at[e], {"wide": source}).wait_recv()
    out_ref[...] = sums[...]
    for copy in sent:
        copy.wait_send()


def update_kernel(ids_ref, summed_ref, table_ref, accum_ref, new_table_ref, new_accum_ref):
    tables, slots = ids_ref.shape
    new_table_ref[...] = table_ref[...]
    new_accum_ref[...] = accum_ref[...]
    for k in range(tables):
        for a in range(slots):
            row = pl.ds(ids_ref[k, a], 1)
            value = summed_ref[k * slots + a:k * slots + a + 1, :]
            grown = accum_ref[k, row, :] + value * value
            new_accum_ref[k, row, :] = grown
            new_table_ref[k, row, :] = table_ref[k, row, :] - learn_rate * value / (
                jnp.sqrt(grown) + epsilon
            )


def shards(n_wide, n_narrow, pooled, cotangent, w_first, b_first, w_second, counts, row_ids, table, accum):
    tables, slots, group_bags = counts.shape
    emb = table.shape[2]
    bags, emb_all = pooled.shape
    shard, inner = w_first.shape
    top = w_second.shape[1]
    pieces = pieces_of(shard, n_wide)
    rows = tables * slots
    span = rows // n_wide
    rest = n_narrow - 1
    groups = tables // max(1, 256 // emb)
    scale = 1.0 / math.sqrt(group_bags)
    limit = clip_factor * math.sqrt(emb)
    hbm = pl.BlockSpec(memory_space=pl.ANY)
    vmem = pl.BlockSpec(memory_space=pltpu.VMEM)
    dma = pltpu.SemaphoreType.DMA
    summed = pl.pallas_call(
        functools.partial(tower_kernel, n_wide, n_narrow, pieces, scale, limit),
        out_shape=jax.ShapeDtypeStruct((n_wide, span, emb), jnp.float32),
        in_specs=[hbm, hbm, hbm, hbm, vmem, hbm],
        out_specs=vmem,
        scratch_shapes=[
            pltpu.VMEM((bags, emb_all), jnp.bfloat16),
            pltpu.VMEM((bags, top), jnp.bfloat16),
            pltpu.VMEM((emb_all, inner), jnp.bfloat16),
            pltpu.VMEM((inner, top), jnp.bfloat16),
            pltpu.VMEM((n_narrow, tables, slots, bags), jnp.bfloat16),
            pltpu.VMEM((bags, inner), jnp.float32),
            pltpu.VMEM((bags, inner), jnp.float32),
            pltpu.VMEM((bags, inner), jnp.bfloat16),
            pltpu.VMEM((n_narrow, rows, emb), jnp.float32),
            pltpu.VMEM((n_narrow, rows, emb), jnp.float32),
            pltpu.VMEM((n_wide, span, emb), jnp.float32),
            pltpu.VMEM((n_wide, span, emb), jnp.float32),
            pltpu.VMEM((n_wide, span, emb), jnp.float32),
            dma((5,)),
            dma((2, rest, pieces)),
            dma((2, rest, pieces)),
            dma((rest,)),
            dma((rest,)),
            dma((rest, groups)),
            dma((rest, groups)),
            dma((n_wide - 1,)),
            dma((n_wide - 1,)),
            dma((n_wide - 1,)),
            dma((n_wide - 1,)),
        ],
        compiler_params=pltpu.CompilerParams(
            collective_id=0, has_side_effects=True, vmem_limit_bytes=56 * 1024 * 1024
        ),
        name="tower",
    )(pooled, cotangent, w_first, w_second, b_first.reshape(1, inner), counts)
    return pl.pallas_call(
        update_kernel,
        out_shape=(
            jax.ShapeDtypeStruct(table.shape, table.dtype),
            jax.ShapeDtypeStruct(accum.shape, accum.dtype),
        ),
        in_specs=[pl.BlockSpec(memory_space=pltpu.SMEM), vmem, vmem, vmem],
        out_specs=(vmem, vmem),
        name="update",
    )(row_ids, summed.reshape(rows, emb), table, accum)


def solution(mesh):
    in_specs = (
        P(("wide", "narrow"), None),
        P(("wide", "narrow"), None),
        P("narrow", None),
        P(),
        P("narrow", None),
        P(None, "narrow", "wide"),
        P(None, "narrow"),
        P(None, "narrow", None),
        P(None, "narrow", None),
    )
    out_specs = (P(None, "narrow", None), P(None, "narrow", None))
    step = functools.partial(shards, mesh.shape["wide"], mesh.shape["narrow"])
    return jax.shard_map(step, mesh=mesh, in_specs=in_specs, out_specs=out_specs, check_vma=False)
```

time: 200 us -> 50.4 us (0.25)
  waiting for transfers between devices: 100 us -> 0 us
  Pallas kernels: 0 us -> 49.6 us
  local copies, waits for them, and re-layouts: 39.3 us -> 0 us
  blocking collectives: 35.4 us -> 0 us
  between operations: 13.9 us -> 0.64 us
  matrix products: 9.06 us -> 0 us
    psum x1 -> x0, waiting for transfers between devices: 50.5 us -> none  [shards(): summed = lax.psum(clipped, 'wide')]
    pallas_call x0 -> x2, Pallas kernels: none -> 49.6 us  [the longest x1 47.4 us: shards(): pl.pallas_call(functools.partial(tower_kernel, n_wide, n_narrow, pieces,...]
    all_to_all x1 -> x0, blocking collectives: 35.4 us -> none  [shards(): lax.all_to_all(counts, 'narrow', split_axis=2, concat_axis=1, tiled=True)]
    all_gather x2 -> x0, waiting for transfers between devices: 29.2 us -> none  [the longest x1 24.1 us: shards(): lax.all_gather(w_second, 'narrow', axis=0, tiled=True)]
    reduce_scatter x1 -> x0, waiting for transfers between devices: 19.5 us -> none  [shards(): lax.psum_scatter(jnp.einsum('tab,btd->atd', regrouped, local_grad, prefer...]
    unnamed x18 -> x0, local copies, waits for them, and re-layouts: 17.7 us -> none
    scatter x2 -> x0, local copies, waits for them, and re-layouts: 13.8 us -> none  [the longest x1 6.9 us: shards(): accum.at[table_index, row_ids].set(jnp.transpose(new_acc, (1, 0, 2)))]
    dot_general x3 -> x0, matrix products: 9.06 us -> none  [the longest x1 4.55 us: tower_back(): lax.dot_general(deltas, w_first, (((1,), (1,)), ((), ())), preferred_elem...]
  transfers between devices with their start and end apart: 4 -> 0, of which waited for: 4 -> 0; matrix products, arithmetic and copies ran while one was open for 13% -> 0% of each run, Pallas kernels for 0% -> 0%
where the time goes in v1:
time: 50.4 us; the launch traced here: 50.2 us
  Pallas kernels  49.6 us (98%)
  between operations  0.64 us (1%)
    pallas_call x1, Pallas kernels, shards(): pl.pallas_call(functools.partial(tower_kernel, n_wide, n_narrow, pieces,...  47.4 us
    pallas_call x1, Pallas kernels, shards(): pl.pallas_call(update_kernel, out_shape=(jax.ShapeDtypeStruct(table.shape...  2.14 us

profile of v1, /device:TPU:0, one launch (start us, length us, event | category | flops | bytes accessed | tf_op | source)
XLA Modules:
  0.0 50.2 jit_solution(7257477665864002554)
XLA Ops:
  0.6 47.4 %tower.1 = f32[8,16,128]{2,1,0:T(8,128)} custom-call(bf16[512,1024]{1,0:T(8,128)(2,1)} %pooled_hbm.1, bf16[512,512]{1,0:T(8,128)(2,1)} %cot_hbm.1, bf16[256,1024]{1,0:T(8,128)(2,1)} %w1_hbm.1, bf16[256,512]{1,0:T(8,128)(2,1)} %w2_hbm.1, f32[1,1024]{1,0:T(1,128)} %bitcast.3, bf16[8,16,2048]{2,1,0:T(8,128)(2,1)} %counts_hbm.1), custom_call_target="tpu_custom_call" | custom-call | tf_op jit(solution)/shard_map/tower/pallas_call | solution.py:305
  48.1 2.1 %update.1 = (f32[8,64,128]{2,1,0:T(8,128)}, f32[8,64,128]{2,1,0:T(8,128)}) custom-call(s32[8,16]{1,0:T(8,128)} %ids_ref.1, f32[128,128]{1,0:T(8,128)} %bitcast.2, f32[8,64,128]{2,1,0:T(8,128)} %table_ref.1, f32[8,64,128]{2,1,0:T(8,128)} %accum_ref.1), custom_call_target="tpu_custom_call" | custom-call | tf_op jit(solution)/shard_map/update/pallas_call | solution.py:341

commit v2 on v1

v2 whole, which is shorter than its diff:
```python
import functools
import math

import jax
import jax.numpy as jnp
from jax import lax
from jax.experimental import pallas as pl
from jax.experimental.pallas import tpu as pltpu
from jax.sharding import PartitionSpec as P

MESH = pl.DeviceIdType.MESH
clip_factor = 0.5
learn_rate = 0.05
epsilon = 1e-08
skew = 3
NT = (((1,), (1,)), ((), ()))


def flip(index, bit):
    return index + bit * (1 - 2 * ((index // bit) % 2))


def pieces_of(shard_rows, n_wide):
    pieces = 1
    while n_wide % (2 * pieces) == 0 and shard_rows % (32 * pieces) == 0:
        pieces *= 2
    return pieces


def masks_of(pieces):
    across = list(range(2, pieces, 2))
    return [masks for masks in (across, [1] if pieces > 1 else []) if masks]


def flips(index, mask):
    bit = 1
    while bit <= mask:
        if mask & bit:
            index = flip(index, bit)
        bit *= 2
    return index


def tower_kernel(
    n_wide, n_narrow, pieces, scale, limit,
    pooled_hbm, cot_hbm, w1_hbm, w2_hbm, bias_ref, counts_hbm, out_ref,
    pooled, cot, w1, w2, looks, hidden, back, deltas, gfull, gsend, grecv, sums,
    local_sem, wsend_sem, wrecv_sem, csend_sem, crecv_sem, gsend_sem, grecv_sem,
    asend_sem, arecv_sem,
):
    wide = lax.axis_index("wide")
    narrow = lax.axis_index("narrow")
    shard = w1_hbm.shape[0]
    piece_rows = shard // pieces
    bags = pooled.shape[0]
    inner = w1.shape[1]
    emb = gfull.shape[3]
    tables, slots = looks.shape[1], looks.shape[2]
    rest = n_narrow - 1
    part = wide % pieces
    base = wide - part
    masks = masks_of(pieces)
    half = inner // 2
    units = [
        (w1, w1_hbm, pl.ds(0, half)),
        (w1, w1_hbm, pl.ds(half, half)),
        (w2, w2_hbm, pl.ds(0, w2.shape[1])),
    ]
    stages = len(masks)

    def lane_block(index, size):
        return pl.ds(pl.multiple_of(index * size, size), size)

    def local(step, src, dst):
        return pltpu.make_async_copy(src, dst, local_sem.at[step])

    own_rows = lane_block(narrow, shard)
    locals_ = [
        local(0, pooled_hbm, pooled),
        local(1, w1_hbm, w1.at[own_rows, :]),
        local(2, cot_hbm, cot),
        local(3, w2_hbm, w2.at[own_rows, :]),
        local(4, counts_hbm.at[:, :, lane_block(narrow, bags)], looks.at[narrow]),
    ]
    for copy in locals_:
        copy.start()

    barrier = pltpu.get_barrier_semaphore()
    for d in range(1, n_narrow):
        pl.semaphore_signal(
            barrier, inc=1, device_id={"narrow": (narrow + d) % n_narrow}, device_id_type=MESH
        )
    for d in range(1, n_wide):
        pl.semaphore_signal(
            barrier, inc=1, device_id={"wide": (wide + d) % n_wide}, device_id_type=MESH
        )
    pl.semaphore_wait(barrier, n_narrow + n_wide - 2)

    def remote(src, dst, send, recv, device):
        return pltpu.make_async_remote_copy(
            src_ref=src, dst_ref=dst, send_sem=send, recv_sem=recv,
            device_id=device, device_id_type=MESH,
        )

    sent = []

    def launch(copy):
        copy.start()
        sent.append(copy)

    def rows_at(source, piece):
        return pl.ds(pl.multiple_of(source * shard + piece * piece_rows, piece_rows), piece_rows)

    for d in range(rest):
        target = {"narrow": (narrow + d + 1) % n_narrow}
        for u, (ref, shard_ref, columns) in enumerate(units):
            launch(remote(
                shard_ref.at[lane_block(part, piece_rows), columns],
                ref.at[rows_at(narrow, part), columns],
                wsend_sem.at[u, d, 0], wrecv_sem.at[u, d, 0], target,
            ))
    for d in range(rest):
        owner = (narrow + d + 1) % n_narrow
        launch(remote(
            counts_hbm.at[:, :, lane_block(owner, bags)], looks.at[narrow],
            csend_sem.at[d], crecv_sem.at[d], {"narrow": owner},
        ))

    held = [[[part] for _ in range(rest)] for _ in units]

    def stage_arrive(u, d, stage):
        source = (narrow + n_narrow - d - 1) % n_narrow
        ref, _, columns = units[u]
        if stage == 0:
            moves = [(part, {"narrow": source})]
            first = 0
        else:
            moves = [
                (flips(q, mask), {"wide": base + flips(part, mask)})
                for mask in masks[stage - 1] for q in held[u][d]
            ]
            first = len(held[u][d])
        for i, (q, device) in enumerate(moves):
            view = ref.at[rows_at(source, q), columns]
            remote(
                view, view, wsend_sem.at[u, d, first + i], wrecv_sem.at[u, d, first + i], device
            ).wait_recv()
        if stage:
            held[u][d] = held[u][d] + [q for q, _ in moves]

    def stage_send(u, d, stage):
        source = (narrow + n_narrow - d - 1) % n_narrow
        ref, _, columns = units[u]
        slot = len(held[u][d])
        for mask in masks[stage]:
            for q in held[u][d]:
                view = ref.at[rows_at(source, q), columns]
                launch(remote(
                    view, view, wsend_sem.at[u, d, slot], wrecv_sem.at[u, d, slot],
                    {"wide": base + flips(part, mask)},
                ))
                slot += 1

    tile = min(256, inner)

    def add_chunk(source, fresh):
        rows = lane_block(source, shard)
        lhs = pooled[:, rows]

        def body(t, carry):
            columns = lane_block(t, tile)
            value = jnp.dot(lhs, w1[rows, columns], preferred_element_type=jnp.float32)
            if fresh:
                hidden[:, columns] = value
            else:
                hidden[:, columns] = hidden[:, columns] + value
            return carry

        lax.fori_loop(0, inner // tile, body, 0)
        back[:, rows] = lax.dot_general(
            cot[...], w2[rows, :], NT, preferred_element_type=jnp.float32
        )

    chunked = shard % 128 == 0
    for copy in locals_:
        copy.wait()
    if chunked:
        add_chunk(narrow, True)
    items = rest * len(units)
    for t in range(items + skew * stages):
        for stage in range(stages + 1):
            item = t - skew * stage
            if 0 <= item < items:
                d, u = divmod(item, len(units))
                stage_arrive(u, d, stage)
                if stage < stages:
                    stage_send(u, d, stage)
                elif chunked and u == len(units) - 1:
                    add_chunk((narrow + n_narrow - d - 1) % n_narrow, False)

    def activate(t, carry):
        columns = lane_block(t, tile)
        if chunked:
            value = hidden[:, columns]
            back_value = back[:, columns]
        else:
            value = jnp.dot(pooled[...], w1[:, columns], preferred_element_type=jnp.float32)
            back_value = lax.dot_general(
                cot[...], w2[columns, :], NT, preferred_element_type=jnp.float32
            )
        value = value + bias_ref[:, columns]
        sig = jax.nn.sigmoid(value)
        slopes = sig * (1.0 + value * (1.0 - sig))
        deltas[:, columns] = (back_value * slopes).astype(jnp.bfloat16)
        return carry

    lax.fori_loop(0, inner // tile, activate, 0)

    for d in range(rest):
        source = (narrow + n_narrow - d - 1) % n_narrow
        view = looks.at[source]
        remote(view, view, csend_sem.at[d], crecv_sem.at[d], {"narrow": source}).wait_recv()

    groups = tables // 2
    for t in range(groups):
        wrows = w1[2 * t * emb:2 * (t + 1) * emb, :]
        grad_in = lax.dot_general(
            deltas[...], wrows, NT, preferred_element_type=jnp.float32
        ).astype(jnp.bfloat16)
        for i in range(2):
            k = 2 * t + i
            lookups = looks[:, k].reshape(n_narrow * slots, bags)
            value = jnp.dot(
                lookups, grad_in[:, i * emb:(i + 1) * emb], preferred_element_type=jnp.float32
            )
            for owner in range(n_narrow):
                rows = value[owner * slots:(owner + 1) * slots]
                gfull[owner, k] = rows
                gsend[owner, k] = rows.astype(jnp.bfloat16)
        block = pl.ds(2 * t, 2)
        for d in range(rest):
            owner = (narrow + d + 1) % n_narrow
            launch(remote(
                gsend.at[owner, block], grecv.at[narrow, block],
                gsend_sem.at[d, t], grecv_sem.at[d, t], {"narrow": owner},
            ))
    for t in range(groups):
        block = pl.ds(2 * t, 2)
        total = gfull[narrow, block]
        for d in range(rest):
            source = (narrow + n_narrow - d - 1) % n_narrow
            view = grecv.at[source, block]
            remote(view, view, gsend_sem.at[d, t], grecv_sem.at[d, t], {"narrow": source}).wait_recv()
            total = total + grecv[source, block].astype(jnp.float32)
        grads = total * scale
        norms = jnp.sqrt(jnp.sum(grads * grads, axis=-1, keepdims=True))
        sums[wide, block] = (grads * (limit / jnp.maximum(norms, limit))).astype(jnp.bfloat16)
        for e in range(n_wide - 1):
            launch(remote(
                sums.at[wide, block], sums.at[wide, block],
                asend_sem.at[t, e], arecv_sem.at[t, e], {"wide": (wide + e + 1) % n_wide},
            ))
    for t in range(groups):
        block = pl.ds(2 * t, 2)
        for e in range(n_wide - 1):
            source = (wide + n_wide - e - 1) % n_wide
            view = sums.at[source, block]
            remote(view, view, asend_sem.at[t, e], arecv_sem.at[t, e], {"wide": source}).wait_recv()
        summed = sums[0, block].astype(jnp.float32)
        for q in range(1, n_wide):
            summed = summed + sums[q, block].astype(jnp.float32)
        out_ref[block] = summed
    for copy in sent:
        copy.wait_send()


def update_kernel(ids_ref, summed_ref, table_ref, accum_ref, new_table_ref, new_accum_ref):
    tables, slots = ids_ref.shape
    new_table_ref[...] = table_ref[...]
    new_accum_ref[...] = accum_ref[...]
    for k in range(tables):
        for a in range(slots):
            row = pl.ds(ids_ref[k, a], 1)
            value = summed_ref[k, a:a + 1, :]
            grown = accum_ref[k, row, :] + value * value
            new_accum_ref[k, row, :] = grown
            new_table_ref[k, row, :] = table_ref[k, row, :] - learn_rate * value / (
                jnp.sqrt(grown) + epsilon
            )


def shards(n_wide, n_narrow, pooled, cotangent, w_first, b_first, w_second, counts, row_ids, table, accum):
    tables, slots, group_bags = counts.shape
    emb = table.shape[2]
    bags, emb_all = pooled.shape
    shard, inner = w_first.shape
    top = w_second.shape[1]
    pieces = pieces_of(shard, n_wide)
    rest = n_narrow - 1
    groups = tables // 2
    scale = 1.0 / math.sqrt(group_bags)
    limit = clip_factor * math.sqrt(emb)
    hbm = pl.BlockSpec(memory_space=pl.ANY)
    vmem = pl.BlockSpec(memory_space=pltpu.VMEM)
    dma = pltpu.SemaphoreType.DMA
    summed = pl.pallas_call(
        functools.partial(tower_kernel, n_wide, n_narrow, pieces, scale, limit),
        out_shape=jax.ShapeDtypeStruct((tables, slots, emb), jnp.float32),
        in_specs=[hbm, hbm, hbm, hbm, vmem, hbm],
        out_specs=vmem,
        scratch_shapes=[
            pltpu.VMEM((bags, emb_all), jnp.bfloat16),
            pltpu.VMEM((bags, top), jnp.bfloat16),
            pltpu.VMEM((emb_all, inner), jnp.bfloat16),
            pltpu.VMEM((inner, top), jnp.bfloat16),
            pltpu.VMEM((n_narrow, tables, slots, bags), jnp.bfloat16),
            pltpu.VMEM((bags, inner), jnp.float32),
            pltpu.VMEM((bags, inner), jnp.float32),
            pltpu.VMEM((bags, inner), jnp.bfloat16),
            pltpu.VMEM((n_narrow, tables, slots, emb), jnp.float32),
            pltpu.VMEM((n_narrow, tables, slots, emb), jnp.bfloat16),
            pltpu.VMEM((n_narrow, tables, slots, emb), jnp.bfloat16),
            pltpu.VMEM((n_wide, tables, slots, emb), jnp.bfloat16),
            dma((5,)),
            dma((3, rest, pieces)),
            dma((3, rest, pieces)),
            dma((rest,)),
            dma((rest,)),
            dma((rest, groups)),
            dma((rest, groups)),
            dma((groups, n_wide - 1)),
            dma((groups, n_wide - 1)),
        ],
        compiler_params=pltpu.CompilerParams(
            collective_id=0, has_side_effects=True, vmem_limit_bytes=56 * 1024 * 1024
        ),
        name="tower",
    )(pooled, cotangent, w_first, w_second, b_first.reshape(1, inner), counts)
    return pl.pallas_call(
        update_kernel,
        out_shape=(
            jax.ShapeDtypeStruct(table.shape, table.dtype),
            jax.ShapeDtypeStruct(accum.shape, accum.dtype),
        ),
        in_specs=[pl.BlockSpec(memory_space=pltpu.SMEM), vmem, vmem, vmem],
        out_specs=(vmem, vmem),
        name="update",
    )(row_ids, summed, table, accum)


def solution(mesh):
    in_specs = (
        P(("wide", "narrow"), None),
        P(("wide", "narrow"), None),
        P("narrow", None),
        P(),
        P("narrow", None),
        P(None, "narrow", "wide"),
        P(None, "narrow"),
        P(None, "narrow", None),
        P(None, "narrow", None),
    )
    out_specs = (P(None, "narrow", None), P(None, "narrow", None))
    step = functools.partial(shards, mesh.shape["wide"], mesh.shape["narrow"])
    return jax.shard_map(step, mesh=mesh, in_specs=in_specs, out_specs=out_specs, check_vma=False)
```

time: 50.4 us -> 45.1 us (0.89)
  Pallas kernels: 49.6 us -> 44.3 us
    pallas_call x1, Pallas kernels: 47.4 us -> 42.2 us  [shards(): pl.pallas_call(functools.partial(tower_kernel, n_wide, n_narrow, pieces,...]
where the time goes in v2:
time: 45.1 us; the launch traced here: 45 us
  Pallas kernels  44.3 us (98%)
  between operations  0.64 us (1%)
    pallas_call x1, Pallas kernels, shards(): pl.pallas_call(functools.partial(tower_kernel, n_wide, n_narrow, pieces,...  42.2 us
    pallas_call x1, Pallas kernels, shards(): pl.pallas_call(update_kernel, out_shape=(jax.ShapeDtypeStruct(table.shape...  2.14 us

profile of v2, /device:TPU:0, one launch (start us, length us, event | category | flops | bytes accessed | tf_op | source)
XLA Modules:
  0.0 45.0 jit_solution(8373791798289210982)
XLA Ops:
  0.6 42.2 %tower.1.summed_ref = f32[8,16,128]{2,1,0:T(8,128)} custom-call(bf16[512,1024]{1,0:T(8,128)(2,1)} %pooled_hbm.1, bf16[512,512]{1,0:T(8,128)(2,1)} %cot_hbm.1, bf16[256,1024]{1,0:T(8,128)(2,1)} %w1_hbm.1, bf16[256,512]{1,0:T(8,128)(2,1)} %w2_hbm.1, f32[1,1024]{1,0:T(1,128)} %bitcast.1, bf16[8,16,2048]{2,1,0:T(8,128)(2,1)} %counts_hbm.1), custom_call_target="tpu_custom_call" | custom-call | tf_op jit(solution)/shard_map/tower/pallas_call | solution.py:306
  42.8 2.1 %update.1 = (f32[8,64,128]{2,1,0:T(8,128)}, f32[8,64,128]{2,1,0:T(8,128)}) custom-call(s32[8,16]{1,0:T(8,128)} %ids_ref.1, f32[8,16,128]{2,1,0:T(8,128)} %tower.1.summed_ref, f32[8,64,128]{2,1,0:T(8,128)} %table_ref.1, f32[8,64,128]{2,1,0:T(8,128)} %accum_ref.1), custom_call_target="tpu_custom_call" | custom-call | tf_op jit(solution)/shard_map/update/pallas_call | solution.py:339
